TPU v7x, 128 devices: a whole 4x4x4 slice. The times are simulated.
128 devices in a mesh: batch: 8 (over y, core), replica: 4 (over x), proto: 4 (over z).
Axes of the slice: x: 4, y: 4, z: 4, core: 2. Of those that a mesh axis runs over, the one named last changes fastest.
Arguments:
- view_one: bfloat16 [16384, 512], P(('batch', 'replica')), may hold values from -4 to 4
- view_two: bfloat16 [16384, 512], P(('batch', 'replica')), may hold values from -4 to 4
- prototypes: bfloat16 [16384, 512], P('proto'), may hold values from -8 to 8
- pairing: int32 [32, 512], P(('batch', 'replica')), may hold values from 0 to 511, as said below
Outputs:
- grad_one: float32 [16384, 512], P(('batch', 'replica'))
- grad_two: float32 [16384, 512], P(('batch', 'replica'))
- grad_prototypes: float32 [16384, 512], P('proto')
Inputs may be any that keep to these rules, and one draw needn't show every extreme that they name: Each row of pairing names every one of 0 to 511 once.
All inputs are finite; a program needn't handle non-finite values.
Results may differ from a plain program's by a relative error of at most 0.0018.
The roundings to bfloat16 on the way count: a program that leaves them out, or rounds other values in their place, can miss the bound.
Values sent between devices are 32-bit elements; how exact they have to be, the bound alone decides.
A program may use at most 128 MiB of HBM per device.

v0:
```python
import jax
import jax.numpy as jnp
from jax import lax
from jax.sharding import PartitionSpec as P

ITERS = 3
sink_eps = 0.05
softness_divisor = 0.1


def unit_rows(x):
    xf = x.astype(jnp.float32)
    inv = lax.rsqrt(jnp.sum(xf * xf, -1, keepdims=True) + 1e-06)
    return (xf * inv, inv)


def unit_back(grad, unit, inv):
    return inv * (grad - unit * jnp.sum(unit * grad, -1, keepdims=True))


def balance_single(similarity_logits):
    codes = jnp.exp(similarity_logits / sink_eps)
    for step in range(ITERS):
        codes = codes / lax.psum(jnp.sum(codes, 0, keepdims=True), ("batch", "replica"))
        codes = codes / lax.psum(jnp.sum(codes, 1, keepdims=True), "proto")
    return codes


def per_device(view_one, view_two, prototypes, pairing):
    unit_one, inv_one = unit_rows(view_one)
    unit_two, inv_two = unit_rows(view_two)
    unit_proto, inv_proto = unit_rows(prototypes)
    low_one = unit_one.astype(jnp.bfloat16)
    low_two = unit_two.astype(jnp.bfloat16)
    low_proto = unit_proto.astype(jnp.bfloat16)
    dims = (((1,), (1,)), ((), ()))
    logits_first_view = lax.dot_general(
        low_one, low_proto, dims, preferred_element_type=jnp.float32
    )
    logits_second_view = lax.dot_general(
        low_two, low_proto, dims, preferred_element_type=jnp.float32
    )
    codes_one = balance_single(logits_first_view)
    codes_two = balance_single(logits_second_view)
    exponent_first_view = jnp.exp(logits_first_view / softness_divisor)
    exponent_second_view = jnp.exp(logits_second_view / softness_divisor)
    total_one, total_two = lax.psum(
        (
            jnp.sum(exponent_first_view, 1, keepdims=True),
            jnp.sum(exponent_second_view, 1, keepdims=True),
        ),
        "proto",
    )
    local_rows = view_one.shape[0]
    partner = pairing[0]
    inverse = (
        jnp.zeros((local_rows,), jnp.int32).at[partner].set(jnp.arange(local_rows, dtype=jnp.int32))
    )
    target_one = codes_two[partner]
    target_two = codes_one[inverse]
    gradient_scale_factor = 0.5 / softness_divisor
    dscore_one = (gradient_scale_factor * (exponent_first_view / total_one - target_one)).astype(
        jnp.bfloat16
    )
    dscore_two = (gradient_scale_factor * (exponent_second_view / total_two - target_two)).astype(
        jnp.bfloat16
    )
    part_one = jnp.dot(dscore_one, low_proto, preferred_element_type=jnp.float32)
    part_two = jnp.dot(dscore_two, low_proto, preferred_element_type=jnp.float32)
    dunit_one, dunit_two = lax.psum((part_one, part_two), "proto")
    grad_one = unit_back(dunit_one, unit_one, inv_one)
    grad_two = unit_back(dunit_two, unit_two, inv_two)
    tdims = (((0,), (0,)), ((), ()))
    local_grad = lax.dot_general(dscore_one, low_one, tdims, preferred_element_type=jnp.float32)
    local_grad = local_grad + lax.dot_general(
        dscore_two, low_two, tdims, preferred_element_type=jnp.float32
    )
    dunit_proto = lax.psum(local_grad, ("batch", "replica"))
    grad_prototypes = unit_back(dunit_proto, unit_proto, inv_proto)
    return (grad_one, grad_two, grad_prototypes)


def solution(mesh):
    placed = (
        P(("batch", "replica"), None),
        P(("batch", "replica"), None),
        P("proto", None),
        P(("batch", "replica"), None),
    )
    return jax.shard_map(
        per_device,
        mesh=mesh,
        in_specs=placed,
        out_specs=(P(("batch", "replica"), None), P(("batch", "replica"), None), P("proto", None)),
        check_vma=False,
    )
```

profile of v0, /device:TPU:1, one launch (start us, length us, event | category | flops | bytes accessed | tf_op | source)
XLA Modules:
  0.0 741.3 jit_solution(12639128571758803586)
XLA Ops:
  7.2 3.1 fusion.18
  12.8 8.5 %fusion.31 = (f32[4096]{0:T(1024)S(1)}, f32[512,4096]{1,0:T(8,128)}) fusion(bf16[4096,512]{1,0:T(8,128)(2,1)} %param.6, f32[4096]{0:T(1024)S(1)} %add_rsqrt_fusion, bf16[512,512]{1,0:T(8,128)(2,1)} %param.5, f32[512]{0:T(512)S(1)} %add_rsqrt_fusion.1), kind=kOutput, calls=%fused_computation.49 | convolution fusion | flops 2158751744 | bytes 13142016 | tf_op jit(solution)/shard_map/dot_general | solution.py:40
  21.3 5.0 fusion.32
  26.2 124.9 %all-reduce.2 = (f32[4096]{0:T(1024)S(1)}, f32[4096]{0:T(1024)S(1)}) all-reduce(f32[4096]{0:T(1024)S(1)} %get-tuple-element.25, f32[4096]{0:T(1024)S(1)} %get-tuple-element.27), channel_id=1, replica_groups=mesh['batch'=8,'replica'=4,'proto'=4] {'batch','replica'}, use_global_device_ids=true, to_apply=%region_6.0 | all-reduce | flops 8192 | bytes 65536 | tf_op jit(solution)/shard_map/psum | solution.py:24
  151.1 8.0 %fusion.30 = (f32[512]{0:T(512)S(1)}, f32[512]{0:T(512)S(1)}, f32[512]{0:T(512)S(1)}) fusion(f32[512,4096]{1,0:T(8,128)} %get-tuple-element.26, f32[4096]{0:T(1024)S(1)} %get-tuple-element.11, f32[4096]{0:T(1024)S(1)} %get-tuple-element.12, f32[512,4096]{1,0:T(8,128)} %get-tuple-element.28), kind=kLoop, calls=%fused_computation.47 | loop fusion | flops 16775680 | bytes 16816128 | tf_op jit(solution)/shard_map/reduce_sum | solution.py:50
  159.1 9.7 %all-reduce.5 = (f32[512]{0:T(512)S(1)}, f32[512]{0:T(512)S(1)}) all-reduce(f32[512]{0:T(512)S(1)} %get-tuple-element.4, f32[512]{0:T(512)S(1)} %get-tuple-element.29), channel_id=1, replica_groups=mesh['batch'=8,'replica'=4,'proto'=4] {'proto'}, use_global_device_ids=true, to_apply=%region_8.0 | all-reduce | flops 1024 | bytes 8192 | tf_op jit(solution)/shard_map/psum | solution.py:25
  168.9 4.7 fusion.22
  173.6 4.7 fusion.21
  178.2 126.6 %all-reduce.1 = (f32[4096]{0:T(1024)S(1)}, f32[4096]{0:T(1024)S(1)}) all-reduce(f32[4096]{0:T(1024)S(1)} %fusion.21, f32[4096]{0:T(1024)S(1)} %fusion.22), channel_id=1, replica_groups=mesh['batch'=8,'replica'=4,'proto'=4] {'batch','replica'}, use_global_device_ids=true, to_apply=%region_10.0 | all-reduce | flops 8192 | bytes 65536 | tf_op jit(solution)/shard_map/psum | solution.py:24
  304.8 4.7 fusion.23
  309.5 4.7 fusion.24
  314.2 6.0 all-reduce.4
  320.2 5.0 fusion.26
  325.2 5.0 fusion.25
  330.1 125.5 %all-reduce = (f32[4096]{0:T(1024)S(1)}, f32[4096]{0:T(1024)S(1)}) all-reduce(f32[4096]{0:T(1024)S(1)} %fusion.25, f32[4096]{0:T(1024)S(1)} %fusion.26), channel_id=1, replica_groups=mesh['batch'=8,'replica'=4,'proto'=4] {'batch','replica'}, use_global_device_ids=true, to_apply=%region_14.0 | all-reduce | flops 8192 | bytes 65536 | tf_op jit(solution)/shard_map/psum | solution.py:24
  455.7 6.4 fusion.27
  462.1 5.3 fusion.28
  467.4 7.8 %all-reduce.3 = (f32[512]{0:T(512)S(1)}, f32[512]{0:T(512)S(1)}, f32[512]{0:T(512)S(1)}, f32[512]{0:T(512)S(1)}) all-reduce(f32[512]{0:T(512)S(1)} %fusion.28, f32[512]{0:T(512)S(1)} %get-tuple-element.6, f32[512]{0:T(512)S(1)} %get-tuple-element.5, ...), channel_id=1, replica_groups=mesh['batch'=8,'replica'=4,'proto'=4] {'proto'}, use_global_device_ids=true, to_apply=%region_16.0 | all-reduce | flops 2048 | bytes 16384 | tf_op jit(solution)/shard_map/psum | solution.py:25
  475.3 7.4 fusion.19
  482.7 2.6 scatter_custom_fusion
  485.3 12.2 %gather_fusion.1 = f32[512,4096]{1,0:T(8,128)} fusion(f32[512,4096]{1,0:T(8,128)} %fusion.19, s32[1024]{0:T(1024)S(1)} %pad_clamp_fusion), kind=kCustom, calls=%fused_computation.1 | custom fusion | bytes 16779264 | tf_op jit(solution)/shard_map/gather | solution.py:60
  497.5 11.4 %multiply_convert_fusion = (bf16[512,4096]{1,0:T(8,128)(2,1)}, f32[512,4096]{1,0:T(8,128)}) fusion(f32[512,4096]{1,0:T(8,128)} %gather_fusion.1, f32[512,4096]{1,0:T(8,128)} %get-tuple-element.26, f32[512]{0:T(512)S(1)} %get-tuple-element.16, f32[512]{0:T(512)S(1)} %get-tuple-element.13, f32[4096]{0:T(1024)S(1)} %get-tuple-element.7, ...), kind=kLoop, calls=%fused_computation.30 | loop fusion | flops 25165824 | bytes 29417472 | tf_op jit(solution)/shard_map/convert_element_type | solution.py:65
  509.0 12.2 %gather_fusion = f32[512,4096]{1,0:T(8,128)} fusion(f32[512,4096]{1,0:T(8,128)} %get-tuple-element.24, s32[1024]{0:T(1024)S(1)} %pad_clamp_fusion.1), kind=kCustom, calls=%fused_computation | custom fusion | bytes 16779264 | tf_op jit(solution)/shard_map/gather | solution.py:59
  521.2 7.3 multiply_convert_fusion.1
  530.5 3.4 fusion.58
  533.9 3.4 fusion.56
  537.4 4.9 fusion.47
  542.3 6.1 convolution_add_fusion
  548.4 48.4 %all-reduce.12.cloned.1.call-done = (f32[512,512]{1,0:T(8,128)}, f32[512,512]{1,0:T(8,128)}) async-done(((f32[512,512]{1,0:T(8,128)}, f32[512,512]{1,0:T(8,128)}), (f32[512,512]{1,0:T(8,128)}, f32[512,512]{1,0:T(8,128)})) %all-reduce.12.cloned.1.call-update) | async-done | bytes 2097168 | tf_op jit(solution)/shard_map/psum | solution.py:70
  604.7 116.6 %all-reduce.10.cloned.1.call-done = f32[4096,512]{1,0:T(8,128)} async-done(((f32[4096,512]{1,0:T(8,128)}), f32[4096,512]{1,0:T(8,128)}) %all-reduce.10.cloned.1.call-update) | async-done | bytes 8388624 | tf_op jit(solution)/shard_map/psum | solution.py:78
  721.3 6.1 fusion.15
  729.6 4.6 fusion.17
  (38 shorter events, 14.7 us)
Async XLA Ops:
  7.2 589.7 %all-reduce.12.cloned.1.call-start = ((), (), s32[]{:S(2)}) async-start(), calls=%async_computation.1 | async-start | bytes 4194304 | tf_op jit(solution)/shard_map/psum | solution.py:70
  12.8 8.5 %copy-start = (bf16[4096,512]{1,0:T(8,128)(2,1)S(1)}, bf16[4096,512]{1,0:T(8,128)(2,1)}, u32[]{:S(2)}) copy-start(bf16[4096,512]{1,0:T(8,128)(2,1)} %param.6) | copy-start | bytes 12582916
  12.8 8.5 %copy-start.7 = (bf16[512,512]{1,0:T(8,128)(2,1)S(1)}, bf16[512,512]{1,0:T(8,128)(2,1)}, u32[]{:S(2)}) copy-start(bf16[512,512]{1,0:T(8,128)(2,1)} %param.4) | copy-start | bytes 1572868
  475.3 7.4 copy-start.9
  521.2 9.3 %copy-start.1 = (bf16[4096,512]{1,0:T(8,128)(2,1)S(1)}, bf16[4096,512]{1,0:T(8,128)(2,1)}, u32[]{:S(2)}) copy-start(bf16[4096,512]{1,0:T(8,128)(2,1)} %param.6) | copy-start | bytes 12582916
  528.5 2.0 copy-start.6
  530.5 3.4 copy-start.4
  537.3 4.9 copy-start.8
  537.4 183.9 %all-reduce.10.cloned.1.call-start = ((), (), s32[]{:S(2)}) async-start(), calls=%async_computation | async-start | bytes 16777216 | tf_op jit(solution)/shard_map/psum | solution.py:78
  537.4 4.9 copy-start.5
  721.3 6.2 copy-start.2
  721.3 8.3 %copy-start.3 = (f32[4096,512]{1,0:T(8,128)S(1)}, f32[4096,512]{1,0:T(8,128)}, u32[]{:S(2)}) copy-start(f32[4096,512]{1,0:T(8,128)} %all-reduce.10.cloned.1.call-done) | copy-start | bytes 25165828
Sparse Core Ops, SparseCore 0:
  537.5 59.2 all-reduce.11
  601.1 120.0 all-reduce.9
where the time goes:
time: 749 us; the launch traced here: 741 us
  blocking collectives  401 us (54%)
  waiting for transfers between devices  165 us (22%)
  other arithmetic  98.8 us (13%)
  local copies, waits for them, and re-layouts  31.2 us (4%)
  matrix products  31.2 us (4%)
  between operations  14.5 us (2%)
    psum x3, blocking collectives, balance_single(): lax.psum(jnp.sum(codes, 0, keepdims=True), ('batch', 'replica'))  377 us
    psum x1, waiting for transfers between devices, per_device(): dunit_proto = lax.psum(local_grad, ('batch', 'replica'))  117 us
    psum x1, waiting for transfers between devices, per_device(): dunit_one, dunit_two = lax.psum((part_one, part_two), 'proto')  48.4 us
    psum x3, blocking collectives, balance_single(): codes = codes / lax.psum(jnp.sum(codes, 1, keepdims=True), 'proto')  23.6 us
    reduce_sum x4, other arithmetic, balance_single(): codes = codes / lax.psum(jnp.sum(codes, 1, keepdims=True), 'proto')  21.2 us
    reduce_sum x4, other arithmetic, balance_single(): jnp.sum(codes, 0, keepdims=True)  19.2 us
  transfers between devices with their start and end apart: 2, of which 2 were waited for; matrix products, arithmetic and copies ran while one was open for 3% of the time, Pallas kernels for 0%

commit v1 on v0

--- a/solution.py
+++ b/solution.py
@@ -6,6 +6,11 @@
 ITERS = 3
 sink_eps = 0.05
 softness_divisor = 0.1
+
+
+def clusters_touch(t0):
+    p_next = jnp.sum(lax.all_gather(t0, axis_name=("batch", "replica")), 0)
+    return p_next
 
 
 def unit_rows(x):
@@ -21,7 +26,7 @@
 def balance_single(similarity_logits):
     codes = jnp.exp(similarity_logits / sink_eps)
     for step in range(ITERS):
-        codes = codes / lax.psum(jnp.sum(codes, 0, keepdims=True), ("batch", "replica"))
+        codes = codes / clusters_touch(jnp.sum(codes, 0, keepdims=True))
         codes = codes / lax.psum(jnp.sum(codes, 1, keepdims=True), "proto")
     return codes
 

time: 749 us -> 644 us (0.86)
  blocking collectives: 401 us -> 296 us
    psum x3 -> x0, blocking collectives: 377 us -> none  [balance_single(): lax.psum(jnp.sum(codes, 0, keepdims=True), ('batch', 'replica'))]
    all_gather x0 -> x6, blocking collectives: none -> 272 us  [clusters_touch(): p_next = jnp.sum(lax.all_gather(t0, axis_name=('batch', 'replica')), 0)]
    reduce_sum x4 -> x10, other arithmetic: 19.2 us -> 19.6 us  [the longest x4 19.2 us: balance_single(): codes = codes / clusters_touch(jnp.sum(codes, 0, keepdims=True))]
where the time goes in v1:
time: 644 us; the launch traced here: 636 us
  blocking collectives  296 us (46%)
  waiting for transfers between devices  164 us (25%)
  other arithmetic  99.1 us (15%)
  local copies, waits for them, and re-layouts  31.7 us (5%)
  matrix products  31 us (5%)
  between operations  14.7 us (2%)
    all_gather x6, blocking collectives, clusters_touch(): p_next = jnp.sum(lax.all_gather(t0, axis_name=('batch', 'replica')), 0)  272 us
    psum x1, waiting for transfers between devices, per_device(): dunit_proto = lax.psum(local_grad, ('batch', 'replica'))  117 us
    psum x1, waiting for transfers between devices, per_device(): dunit_one, dunit_two = lax.psum((part_one, part_two), 'proto')  47.1 us
    psum x3, blocking collectives, balance_single(): codes = codes / lax.psum(jnp.sum(codes, 1, keepdims=True), 'proto')  23.6 us
    reduce_sum x4, other arithmetic, balance_single(): codes = codes / lax.psum(jnp.sum(codes, 1, keepdims=True), 'proto')  21.2 us
    reduce_sum x4, other arithmetic, balance_single(): codes = codes / clusters_touch(jnp.sum(codes, 0, keepdims=True))  19.2 us
  transfers between devices with their start and end apart: 2, of which 2 were waited for; matrix products, arithmetic and copies ran while one was open for 3% of the time, Pallas kernels for 0%

profile of v1, /device:TPU:1, one launch (start us, length us, event | category | flops | bytes accessed | tf_op | source)
XLA Modules:
  0.0 636.0 jit_solution(9008932449951717306)
XLA Ops:
  12.8 8.3 %fusion.32 = (f32[4096]{0:T(1024)S(1)}, f32[512,4096]{1,0:T(8,128)}) fusion(bf16[4096,512]{1,0:T(8,128)(2,1)} %param.6, f32[4096]{0:T(1024)S(1)} %add_rsqrt_fusion, bf16[512,512]{1,0:T(8,128)(2,1)} %param.4, f32[512]{0:T(512)S(1)} %add_rsqrt_fusion.2), kind=kOutput, calls=%fused_computation.50 | convolution fusion | flops 2158751744 | bytes 13142016 | tf_op jit(solution)/shard_map/dot_general | solution.py:42
  21.1 4.9 fusion.31
  26.0 44.3 %all-gather = f32[131072]{0:T(1024)S(1)} all-gather(f32[4096]{0:T(1024)S(1)} %get-tuple-element.19), channel_id=2, replica_groups=mesh['batch'=8,'replica'=4,'proto'=4] {'batch','replica'}, dimensions={0}, use_global_device_ids=true | all-gather | bytes 540672 | tf_op jit(solution)/shard_map/all_gather | solution.py:12
  70.5 42.0 %all-gather.3 = f32[131072]{0:T(1024)S(1)} all-gather(f32[4096]{0:T(1024)S(1)} %get-tuple-element.21), channel_id=5, replica_groups=mesh['batch'=8,'replica'=4,'proto'=4] {'batch','replica'}, dimensions={0}, use_global_device_ids=true | all-gather | bytes 540672 | tf_op jit(solution)/shard_map/all_gather | solution.py:12
  112.7 8.0 %fusion.30 = (f32[512]{0:T(512)S(1)}, f32[512]{0:T(512)S(1)}, f32[512]{0:T(512)S(1)}) fusion(f32[512,4096]{1,0:T(8,128)} %get-tuple-element.20, f32[4096]{0:T(1024)S(1)} %reduce.6, f32[4096]{0:T(1024)S(1)} %reduce.9, f32[512,4096]{1,0:T(8,128)} %get-tuple-element.22), kind=kLoop, calls=%fused_computation.47 | loop fusion | flops 16775680 | bytes 16816128 | tf_op jit(solution)/shard_map/reduce_sum | solution.py:55
  120.7 9.7 %all-reduce.2 = (f32[512]{0:T(512)S(1)}, f32[512]{0:T(512)S(1)}) all-reduce(f32[512]{0:T(512)S(1)} %get-tuple-element.4, f32[512]{0:T(512)S(1)} %get-tuple-element.23), channel_id=1, replica_groups=mesh['batch'=8,'replica'=4,'proto'=4] {'proto'}, use_global_device_ids=true, to_apply=%region_8.0 | all-reduce | flops 1024 | bytes 8192 | tf_op jit(solution)/shard_map/psum | solution.py:30
  130.5 4.7 fusion.22
  135.1 45.6 %all-gather.4 = f32[131072]{0:T(1024)S(1)} all-gather(f32[4096]{0:T(1024)S(1)} %fusion.22), channel_id=6, replica_groups=mesh['batch'=8,'replica'=4,'proto'=4] {'batch','replica'}, dimensions={0}, use_global_device_ids=true | all-gather | bytes 540672 | tf_op jit(solution)/shard_map/all_gather | solution.py:12
  180.9 4.7 fusion.23
  185.6 4.7 fusion.21
  190.3 42.0 %all-gather.1 = f32[131072]{0:T(1024)S(1)} all-gather(f32[4096]{0:T(1024)S(1)} %fusion.21), channel_id=3, replica_groups=mesh['batch'=8,'replica'=4,'proto'=4] {'batch','replica'}, dimensions={0}, use_global_device_ids=true | all-gather | bytes 540672 | tf_op jit(solution)/shard_map/all_gather | solution.py:12
  232.5 4.7 fusion.24
  237.2 6.0 all-reduce.1
  243.2 5.0 fusion.26
  248.1 45.1 %all-gather.5 = f32[131072]{0:T(1024)S(1)} all-gather(f32[4096]{0:T(1024)S(1)} %fusion.26), channel_id=7, replica_groups=mesh['batch'=8,'replica'=4,'proto'=4] {'batch','replica'}, dimensions={0}, use_global_device_ids=true | all-gather | bytes 540672 | tf_op jit(solution)/shard_map/all_gather | solution.py:12
  293.4 6.4 %fusion.27 = (f32[512]{0:T(512)S(1)}, f32[512]{0:T(512)S(1)}) fusion(f32[4096]{0:T(1024)S(1)} %reduce.11, f32[512]{0:T(512)S(1)} %get-tuple-element.12, f32[4096]{0:T(1024)S(1)} %reduce.10, f32[512]{0:T(512)S(1)} %get-tuple-element.14, f32[4096]{0:T(1024)S(1)} %reduce.9, f32[512,4096]{1,0:T(8,128)} %get-tuple-element.22), kind=kLoop, calls=%fused_computation.44 | loop fusion | flops 18873344 | bytes 8445952 | tf_op jit(solution)/shard_map/reduce_sum | solution.py:30
  299.8 5.0 fusion.25
  304.8 53.2 %all-gather.2 = f32[131072]{0:T(1024)S(1)} all-gather(f32[4096]{0:T(1024)S(1)} %fusion.25), channel_id=4, replica_groups=mesh['batch'=8,'replica'=4,'proto'=4] {'batch','replica'}, dimensions={0}, use_global_device_ids=true | all-gather | bytes 540672 | tf_op jit(solution)/shard_map/all_gather | solution.py:12
  358.2 5.3 fusion.28
  363.5 7.8 %all-reduce = (f32[512]{0:T(512)S(1)}, f32[512]{0:T(512)S(1)}, f32[512]{0:T(512)S(1)}, f32[512]{0:T(512)S(1)}) all-reduce(f32[512]{0:T(512)S(1)} %fusion.28, f32[512]{0:T(512)S(1)} %get-tuple-element.6, f32[512]{0:T(512)S(1)} %get-tuple-element.5, f32[512]{0:T(512)S(1)} %get-tuple-element.3), channel_id=1, replica_groups=mesh['batch'=8,'replica'=4,'proto'=4] {'proto'}, use_global_device_ids=true, to_apply=%region_16.0 | all-reduce | flops 2048 | bytes 16384 | tf_op jit(solution)/shard_map/psum | solution.py:30
  371.3 7.4 %fusion.19 = f32[512,4096]{1,0:T(8,128)} fusion(f32[512]{0:T(512)S(1)} %get-tuple-element.9, f32[4096]{0:T(1024)S(1)} %reduce.11, f32[512]{0:T(512)S(1)} %get-tuple-element.12, f32[4096]{0:T(1024)S(1)} %reduce.10, f32[512]{0:T(512)S(1)} %get-tuple-element.14, f32[4096]{0:T(1024)S(1)} %reduce.9, f32[512,4096]{1,0:T(8,128)} %get-tuple-element.22), kind=kLoop, calls=%fused_computation.28 | loop fusion | flops 14680064 | bytes 16832512 | tf_op jit(solution)/shard_map/div | solution.py:30
  381.2 12.2 %gather_fusion.1 = f32[512,4096]{1,0:T(8,128)} fusion(f32[512,4096]{1,0:T(8,128)} %fusion.19, s32[1024]{0:T(1024)S(1)} %pad_clamp_fusion), kind=kCustom, calls=%fused_computation.1 | custom fusion | bytes 16779264 | tf_op jit(solution)/shard_map/gather | solution.py:65
  393.4 11.4 %multiply_convert_fusion = (bf16[512,4096]{1,0:T(8,128)(2,1)}, f32[512,4096]{1,0:T(8,128)}) fusion(f32[512,4096]{1,0:T(8,128)} %gather_fusion.1, f32[512,4096]{1,0:T(8,128)} %get-tuple-element.20, f32[512]{0:T(512)S(1)} %get-tuple-element.10, f32[512]{0:T(512)S(1)} %get-tuple-element.7, f32[4096]{0:T(1024)S(1)} %reduce.8, f32[512]{0:T(512)S(1)} %get-tuple-element.11, ...), kind=kLoop, calls=%fused_computation.30 | loop fusion | flops 25165824 | bytes 29417472 | tf_op jit(solution)/shard_map/convert_element_type | solution.py:70
  404.8 12.2 %gather_fusion = f32[512,4096]{1,0:T(8,128)} fusion(f32[512,4096]{1,0:T(8,128)} %get-tuple-element.18, s32[1024]{0:T(1024)S(1)} %pad_clamp_fusion.1), kind=kCustom, calls=%fused_computation | custom fusion | bytes 16779264 | tf_op jit(solution)/shard_map/gather | solution.py:64
  417.0 7.3 %multiply_convert_fusion.1 = bf16[512,4096]{1,0:T(8,128)(2,1)S(1)} fusion(f32[512,4096]{1,0:T(8,128)} %gather_fusion, f32[512,4096]{1,0:T(8,128)} %get-tuple-element.22, f32[512]{0:T(512)S(1)} %get-tuple-element.8), kind=kLoop, calls=%fused_computation.33 | loop fusion | flops 10485760 | bytes 20973568 | tf_op jit(solution)/shard_map/convert_element_type | solution.py:67
  429.8 3.4 fusion.56
  433.3 4.9 fusion.47
  438.2 6.1 convolution_add_fusion
  444.3 47.1 %all-reduce.9.cloned.1.call-done = (f32[512,512]{1,0:T(8,128)}, f32[512,512]{1,0:T(8,128)}) async-done(((f32[512,512]{1,0:T(8,128)}, f32[512,512]{1,0:T(8,128)}), (f32[512,512]{1,0:T(8,128)}, f32[512,512]{1,0:T(8,128)})) %all-reduce.9.cloned.1.call-update) | async-done | bytes 2097168 | tf_op jit(solution)/shard_map/psum | solution.py:75
  499.3 116.6 %all-reduce.7.cloned.1.call-done = f32[4096,512]{1,0:T(8,128)} async-done(((f32[4096,512]{1,0:T(8,128)}), f32[4096,512]{1,0:T(8,128)}) %all-reduce.7.cloned.1.call-update) | async-done | bytes 8388624 | tf_op jit(solution)/shard_map/psum | solution.py:83
  615.9 6.1 fusion.15
  624.2 4.6 fusion.17
  (53 shorter events, 24.5 us)
Async XLA Ops:
  7.2 484.2 %all-reduce.9.cloned.1.call-start = ((), (), s32[]{:S(2)}) async-start(), calls=%async_computation.1 | async-start | bytes 4194304 | tf_op jit(solution)/shard_map/psum | solution.py:75
  12.8 8.3 %copy-start = (bf16[4096,512]{1,0:T(8,128)(2,1)S(1)}, bf16[4096,512]{1,0:T(8,128)(2,1)}, u32[]{:S(2)}) copy-start(bf16[4096,512]{1,0:T(8,128)(2,1)} %param.6) | copy-start | bytes 12582916
  12.8 8.3 %copy-start.8 = (bf16[512,512]{1,0:T(8,128)(2,1)S(1)}, bf16[512,512]{1,0:T(8,128)(2,1)}, u32[]{:S(2)}) copy-start(bf16[512,512]{1,0:T(8,128)(2,1)} %param.5) | copy-start | bytes 1572868
  371.3 7.4 %copy-start.9 = (s32[1,512]{1,0:T(1,128)S(1)}, s32[1,512]{1,0:T(1,128)}, u32[]{:S(2)}) copy-start(s32[1,512]{1,0:T(1,128)} %param.7) | copy-start | bytes 6148
  417.0 9.3 %copy-start.1 = (bf16[4096,512]{1,0:T(8,128)(2,1)S(1)}, bf16[4096,512]{1,0:T(8,128)(2,1)}, u32[]{:S(2)}) copy-start(bf16[4096,512]{1,0:T(8,128)(2,1)} %param.6) | copy-start | bytes 12582916
  424.3 2.0 copy-start.6
  426.4 3.4 copy-start.4
  429.8 3.5 copy-start.7
  433.2 182.6 %all-reduce.7.cloned.1.call-start = ((), (), s32[]{:S(2)}) async-start(), calls=%async_computation | async-start | bytes 16777216 | tf_op jit(solution)/shard_map/psum | solution.py:83
  433.3 4.9 copy-start.5
  615.8 6.1 copy-start.2
  615.8 8.3 %copy-start.3 = (f32[4096,512]{1,0:T(8,128)S(1)}, f32[4096,512]{1,0:T(8,128)}, u32[]{:S(2)}) copy-start(f32[4096,512]{1,0:T(8,128)} %all-reduce.7.cloned.1.call-done) | copy-start | bytes 25165828
Sparse Core Ops, SparseCore 0:
  433.4 57.9 all-reduce.8
  495.7 120.0 all-reduce.6
